TPU v7x, 128 devices: a whole 4x4x4 slice. The times are simulated.
128 devices in a mesh: req: 4 (over y), exp: 32 (over z, x, core).
Axes of the slice: x: 4, y: 4, z: 4, core: 2. Of those that a mesh axis runs over, the one named last changes fastest.
Arguments:
- hidden: bfloat16 [8, 2048, 2048], P('req', 'exp'), may hold values from -6 to 6
- q_new: bfloat16 [8, 16, 2048, 128], P('req', None, 'exp'), may hold values from -480 to 480
- k_new: bfloat16 [8, 16, 2048, 128], P('req', None, 'exp'), may hold values from -6 to 6
- v_new: bfloat16 [8, 16, 2048, 128], P('req', None, 'exp'), may hold values from -6 to 6
- routes: int32 [8, 2048, 6], P('req', 'exp'), may hold values from 0 to 63, all different within a row; in each aligned block of 64 rows (0 to 63, 64 to 127, ..., all dimensions but the last counted through in order) at most 8 rows name the same one
- slot_request: int32 [8], replicated, may hold values from 0 to 7, each once
- lengths: int32 [8], replicated, may hold values from 5 to 16384, as said below
- cycle_cache: bfloat16 [128, 2, 4096, 128], P(('req', 'exp')), may hold values from -6 to 6
- sink_cache: bfloat16 [128, 2, 4, 128], P(('req', 'exp')), may hold values from -6 to 6
- w_out: bfloat16 [2048, 2048], replicated, may hold values from -0.125 to 0.125
- norm_gain: float32 [2048], replicated, may hold values from 0.5 to 1.5
- router: bfloat16 [2048, 64], replicated, may hold values from -0.125 to 0.125
- w_gate: bfloat16 [2048, 90112], P(None, ('req', 'exp')), may hold values from -0.125 to 0.125
- w_up: bfloat16 [2048, 90112], P(None, ('req', 'exp')), may hold values from -0.125 to 0.125
- w_down: bfloat16 [90112, 2048], P(('req', 'exp')), may hold values from -0.15625 to 0.15625
Outputs:
- layer_out: bfloat16 [8, 2048, 2048], P('req', 'exp')
- cycle_out: bfloat16 [128, 2, 4096, 128], P(('req', 'exp'))
Inputs may be any that keep to these rules, and one draw needn't show every extreme that they name: In every aligned block of 64 rows of routes (the rows of one request on one index of exp) no expert is named by more than 8 rows, a bound that some block reaches. `slot_request`: each request once. `lengths`: some slot has exactly 16384 cached tokens, and some other fewer than 2048.
All inputs are finite; a program needn't handle non-finite values.
Results may differ from a plain program's by a relative error of at most 0.014.
The roundings to bfloat16 on the way count: a program that leaves them out, or rounds other values in their place, can miss the bound.
Values may be sent and summed in bfloat16 or wider, within the bound.
No kernel may reach another device: no remote copies, remote signals or barrier semaphores. Data moves between devices by JAX's collectives and lax.ppermute only.
A program may use at most 192 MiB of HBM per device.

v0:
```python
import jax
import jax.numpy as jnp
from jax import lax
from jax.sharding import PartitionSpec as P

SPLIT = 2


def for_sending(array):

    def short(part):
        return part.astype(jnp.bfloat16) if part.dtype == jnp.float32 else part

    return jax.tree.map(short, array)


def rotate(vectors, positions):
    half_width = vectors.shape[-1] // 2
    frequency = 10000.0 ** (-2.0 * jnp.arange(half_width, dtype=jnp.float32) / vectors.shape[-1])
    angles = positions.astype(jnp.float32)[:, None] * frequency[None, :]
    cosine = jnp.cos(angles)
    sine_part = jnp.sin(angles)
    low_half = vectors[..., :half_width]
    high_half = vectors[..., half_width:]
    return jnp.concatenate(
        [low_half * cosine - high_half * sine_part, high_half * cosine + low_half * sine_part],
        axis=-1,
    )


def attend_block(
    q_block, row_start, cycle_from, new_upto, ordered, k_rot, value_new, sink_pair, length
):
    window = ordered.shape[1]
    score_scale = q_block.shape[1] ** (-0.5)
    key_rows = jnp.concatenate([ordered[0, cycle_from:], k_rot], 0)
    value_rows = jnp.concatenate([ordered[1, cycle_from:], value_new], 0)
    row_ids = row_start + jnp.arange(q_block.shape[0], dtype=jnp.int32)
    cycle_cols = cycle_from + jnp.arange(window - cycle_from, dtype=jnp.int32)
    cycle_visible = (cycle_cols[None, :] > row_ids[:, None]) & (
        cycle_cols[None, :] >= window - length
    )
    new_visible = jnp.arange(new_upto, dtype=jnp.int32)[None, :] <= row_ids[:, None]
    visible = jnp.concatenate([cycle_visible, new_visible], 1)
    scores = (
        jnp.einsum("qd,kd->qk", q_block, key_rows, preferred_element_type=jnp.float32) * score_scale
    )
    scores = jnp.where(visible, scores, -jnp.inf)
    sink_scores = (
        jnp.einsum("qd,kd->qk", q_block, sink_pair[0], preferred_element_type=jnp.float32)
        * score_scale
    )
    sink_visible = (
        jnp.arange(sink_pair.shape[1], dtype=jnp.int32)[None, :]
        <= (length + row_ids - window)[:, None]
    )
    sink_scores = jnp.where(sink_visible, sink_scores, -jnp.inf)
    highest = jnp.maximum(jnp.max(scores, axis=1), jnp.max(sink_scores, axis=1))[:, None]
    weights = jnp.exp(scores - highest)
    sink_weights = jnp.exp(sink_scores - highest)
    denominator = jnp.sum(weights, axis=1) + jnp.sum(sink_weights, axis=1)
    blended = jnp.dot(weights.astype(jnp.bfloat16), value_rows, preferred_element_type=jnp.float32)
    blended = blended + jnp.dot(
        sink_weights.astype(jnp.bfloat16), sink_pair[1], preferred_element_type=jnp.float32
    )
    return (blended / denominator[:, None]).astype(jnp.bfloat16)


def attend_pair(query_rows, key_new, value_new, cycle_pair, sink_pair, length):
    seq_len = query_rows.shape[0]
    window = cycle_pair.shape[1]
    block_rows = min(512, seq_len)
    positions = length + jnp.arange(seq_len, dtype=jnp.int32)
    q_rot = rotate(query_rows.astype(jnp.float32), positions).astype(jnp.bfloat16)
    k_rot = rotate(key_new.astype(jnp.float32), positions).astype(jnp.bfloat16)
    ordered = jnp.roll(cycle_pair, -(length % window), axis=1)
    outputs = []
    for block_number in range(seq_len // block_rows):
        row_start = block_number * block_rows
        cycle_from = 0
        outputs.append(
            attend_block(
                q_rot[row_start : row_start + block_rows],
                row_start,
                cycle_from,
                seq_len,
                ordered,
                k_rot,
                value_new,
                sink_pair,
                length,
            )
        )
    context = jnp.concatenate(outputs, 0)
    retained = ordered[:, seq_len:]
    appended = jnp.stack([k_rot, value_new])
    updated = jnp.roll(
        jnp.concatenate([retained, appended], 1), (length + seq_len) % window, axis=1
    )
    return (context, updated)


def on_device(
    hidden,
    q_new,
    k_new,
    v_new,
    routes,
    slot_request,
    lengths,
    cycle_cache,
    sink_cache,
    w_out,
    norm_gain,
    router,
    w_gate,
    w_up,
    w_down,
):
    group_width = lax.axis_size("exp")
    group_count = lax.axis_size("req")
    devices_all = group_count * group_width
    group_index = lax.axis_index("req")
    member_index = lax.axis_index("exp")
    slots_here, local_rows, model_width = hidden.shape
    head_count = q_new.shape[1]
    head_dim = q_new.shape[3]
    experts_all = router.shape[1]
    arrived = (
        lax.all_gather(hidden, "req", axis=0, tiled=True),
        lax.all_gather(q_new, "req", axis=0, tiled=True),
        lax.all_gather(k_new, "req", axis=0, tiled=True),
        lax.all_gather(v_new, "req", axis=0, tiled=True),
        lax.all_gather(routes, "req", axis=0, tiled=True),
    )
    requests = lax.dynamic_slice_in_dim(slot_request, group_index * slots_here, slots_here)
    hidden_sel, query_sel, key_sel, value_sel, route_sel = [
        jnp.take(arrival, requests, axis=0) for arrival in arrived
    ]
    pair_count = slots_here * head_count
    query_pairs, key_pairs, value_pairs = (
        lax.all_to_all(
            query_sel.reshape(pair_count, local_rows, head_dim),
            "exp",
            split_axis=0,
            concat_axis=1,
            tiled=True,
        ),
        lax.all_to_all(
            key_sel.reshape(pair_count, local_rows, head_dim),
            "exp",
            split_axis=0,
            concat_axis=1,
            tiled=True,
        ),
        lax.all_to_all(
            value_sel.reshape(pair_count, local_rows, head_dim),
            "exp",
            split_axis=0,
            concat_axis=1,
            tiled=True,
        ),
    )
    pairs_here = pair_count // group_width
    pair_ids = member_index * pairs_here + jnp.arange(pairs_here, dtype=jnp.int32)
    pair_lengths = jnp.take(lengths, group_index * slots_here + pair_ids // head_count)
    context, cycle_out = lax.map(
        lambda packed: attend_pair(*packed),
        (query_pairs, key_pairs, value_pairs, cycle_cache, sink_cache, pair_lengths),
    )
    context_rows = jax.tree.map(
        lambda part, own: part.astype(own.dtype),
        lax.all_to_all(for_sending(context), "exp", split_axis=1, concat_axis=0, tiled=True),
        context,
    ).reshape(slots_here, head_count, local_rows, head_dim)
    projected = jnp.einsum(
        "shqd,hde->sqe",
        context_rows,
        w_out.reshape(head_count, head_dim, model_width),
        preferred_element_type=jnp.float32,
    )
    residual = hidden_sel.astype(jnp.float32) + projected
    inverse = lax.rsqrt(jnp.mean(residual * residual, axis=-1, keepdims=True) + 1e-06)
    normed = (residual * inverse * norm_gain).astype(jnp.bfloat16)
    logits = jnp.einsum("sqd,de->sqe", normed, router, preferred_element_type=jnp.float32)
    gates = jax.nn.softmax(jnp.take_along_axis(logits, route_sel, axis=2), axis=-1)
    most_slots = max(2, local_rows // 8)
    expert_ids = jnp.arange(experts_all, dtype=jnp.int32)
    per_row = jnp.any(route_sel[..., None] == expert_ids, axis=2).astype(jnp.int32)
    earlier = jnp.cumsum(per_row, axis=1) - per_row
    ranks = jnp.take_along_axis(earlier, route_sel, axis=2)
    slot_ids = jnp.broadcast_to(
        jnp.arange(slots_here, dtype=jnp.int32)[:, None, None], route_sel.shape
    )
    spread = jnp.broadcast_to(normed[:, :, None, :], route_sel.shape + (model_width,))
    buffer = (
        jnp.zeros((experts_all, slots_here, most_slots, model_width), jnp.bfloat16)
        .at[route_sel, slot_ids, ranks]
        .set(spread)
    )
    sub_here = experts_all * SPLIT // devices_all
    piece_shape = (devices_all, sub_here, slots_here, most_slots, model_width)
    half_units = w_gate.shape[1] // sub_here
    gate_local = w_gate.reshape(model_width, sub_here, half_units)
    up_local = w_up.reshape(model_width, sub_here, half_units)
    down_local = w_down.reshape(sub_here, half_units, model_width)
    outgoing = jnp.broadcast_to(
        buffer[:, None], (experts_all, SPLIT, slots_here, most_slots, model_width)
    ).reshape(piece_shape)
    received = lax.all_to_all(outgoing, ("req", "exp"), split_axis=0, concat_axis=0, tiled=True)
    gate_part = jnp.einsum(
        "nsrkd,dsf->nsrkf", received, gate_local, preferred_element_type=jnp.float32
    )
    up_part = jnp.einsum("nsrkd,dsf->nsrkf", received, up_local, preferred_element_type=jnp.float32)
    active = (jax.nn.silu(gate_part) * up_part).astype(jnp.bfloat16)
    returned = lax.all_to_all(
        jnp.einsum(
            "nsrkf,sfd->nsrkd", active, down_local, preferred_element_type=jnp.float32
        ).astype(jnp.bfloat16),
        ("req", "exp"),
        split_axis=0,
        concat_axis=0,
        tiled=True,
    )
    pieces = returned.reshape(experts_all, SPLIT, slots_here, most_slots, model_width).astype(
        jnp.float32
    )
    summed = jnp.sum(pieces, axis=1)
    picked = summed[route_sel, slot_ids, ranks]
    moe = jnp.sum(gates[..., None] * picked, axis=2)
    layer_out = (residual + moe).astype(jnp.bfloat16)
    return (layer_out, cycle_out)


def solution(mesh):
    in_specs = (
        P("req", "exp", None),
        P("req", None, "exp", None),
        P("req", None, "exp", None),
        P("req", None, "exp", None),
        P("req", "exp", None),
        P(),
        P(),
        P(("req", "exp"), None, None, None),
        P(("req", "exp"), None, None, None),
        P(),
        P(),
        P(),
        P(None, ("req", "exp")),
        P(None, ("req", "exp")),
        P(("req", "exp"), None),
    )
    out_specs = (P("req", "exp", None), P(("req", "exp"), None, None, None))
    return jax.shard_map(
        on_device, mesh=mesh, in_specs=in_specs, out_specs=out_specs, check_vma=False
    )
```

profile of v0, /device:TPU:10, one launch (start us, length us, event | category | flops | bytes accessed | tf_op | source)
XLA Modules:
  0.0 760.2 jit_solution(11624940726540011022)
XLA Ops:
  14.7 12.3 %all_gather.19 = s32[8,64,6]{1,2,0:T(8,128)S(1)} all-gather(s32[2,64,6]{1,2,0:T(8,128)S(1)} %copy.55), channel_id=1, replica_groups=mesh['req'=4,'exp'=32] {'req'}, dimensions={0}, use_global_device_ids=true | all-gather | bytes 15360 | tf_op jit(solution)/shard_map/all_gather | solution.py:134
  37.7 8.3 %fusion.13 = (pred[512,4096]{1,0:T(32,128)(4,1)}, pred[512,4096]{1,0:T(32,128)(4,1)}, pred[512,4096]{1,0:T(32,128)(4,1)}, pred[512,4096]{1,0:T(32,128)(4,1)}) fusion(pred[4096]{0:T(1024)(128)(4,1)S(1)} %iota_compare_fusion.9, s32[512]{0:T(512)S(1)} %iota_add_fusion.2, s32[512]{0:T(512)S(1)} %get-tuple-element.90, s32[512]{0:T(512)S(1)} %get-tuple-element.89), kind=kLoop, calls=%fused_computation.37 | loop fusion | flops 16777216 | bytes 8398848 | tf_op jit(solution)/shard_map/while/body/eval_jaxpr/and | solution.py:40
  48.2 26.1 %all-gather.9.cloned.1.call-done = bf16[8,16,64,128]{3,2,1,0:T(8,128)(2,1)} async-done(((bf16[2,16,64,128]{3,2,1,0:T(8,128)(2,1)}), bf16[8,16,64,128]{3,2,1,0:T(8,128)(2,1)}) %all-gather.9.cloned.1.call-update) | async-done | bytes 2097168 | tf_op jit(solution)/shard_map/all_gather | solution.py:132
  77.3 29.5 %all-gather.7.cloned.1.call-done = bf16[8,16,64,128]{3,2,1,0:T(8,128)(2,1)} async-done(((bf16[2,16,64,128]{3,2,1,0:T(8,128)(2,1)}), bf16[8,16,64,128]{3,2,1,0:T(8,128)(2,1)}) %all-gather.7.cloned.1.call-update) | async-done | bytes 2097168 | tf_op jit(solution)/shard_map/all_gather | solution.py:131
  112.3 7.6 all-to-all-start.1
  121.5 8.7 %all-to-all-done.1 = bf16[32,64,128]{2,1,0:T(8,128)(2,1)S(1)} async-done(((bf16[32,64,128]{2,1,0:T(8,128)(2,1)}), bf16[32,64,128]{2,1,0:T(8,128)(2,1)S(1)}, u32[]{:S(2)}, u32[]{:S(2)}) %all-to-all-start.1) | async-done | bytes 524320 | tf_op jit(solution)/shard_map/all_to_all | solution.py:149
  137.0 9.4 %all-to-all-done = bf16[32,64,128]{2,1,0:T(8,128)(2,1)} async-done(((bf16[32,64,128]{2,1,0:T(8,128)(2,1)}), bf16[32,64,128]{2,1,0:T(8,128)(2,1)}, u32[]{:S(2)}, u32[]{:S(2)}) %all-to-all-start) | async-done | bytes 524320 | tf_op jit(solution)/shard_map/all_to_all | solution.py:142
  152.6 7.5 fusion.78
  171.0 7.5 fusion.19
  186.9 8.4 %fusion.143 = (f32[512]{0:T(512)S(1)}, f32[512,6144]{1,0:T(8,128)S(1)}) fusion(bf16[512,128]{1,0:T(8,128)(2,1)S(1)} %copy-done.21, bf16[2048,64]{1,0:T(8,128)(2,1)} %copy-done.12, bf16[2048,64]{1,0:T(8,128)(2,1)S(1)} %copy-done.11, bf16[4096,128]{1,0:T(8,128)(2,1)} %get-tuple-element.45, pred[512,2048]{1,0:T(32,128)(4,1)} %iota_compare_fusion.6, ...), kind=kOutput, calls=%fused_computation.234 | convolution fusion | flops 822607360 | bytes 17434624 | tf_op jit(solution)/shard_map/while/body/eval_jaxpr/qd,kd->qk/dot_general | solution.py:46
  197.4 8.6 %fusion.145 = (f32[512]{0:T(512)S(1)}, f32[512,6144]{1,0:T(8,128)}) fusion(bf16[512,128]{1,0:T(8,128)(2,1)S(1)} %copy-done.20, bf16[2048,64]{1,0:T(8,128)(2,1)} %copy-done.12, bf16[2048,64]{1,0:T(8,128)(2,1)S(1)} %copy-done.11, bf16[4096,128]{1,0:T(8,128)(2,1)} %get-tuple-element.45, pred[512,2048]{1,0:T(32,128)(4,1)} %iota_compare_fusion.7, ...), kind=kOutput, calls=%fused_computation.236 | convolution fusion | flops 822607360 | bytes 17434624 | tf_op jit(solution)/shard_map/while/body/eval_jaxpr/qd,kd->qk/dot_general | solution.py:46
  220.0 8.9 %copy.87 = bf16[1,2048,128]{2,0,1:T(2,128)(2,1)} copy(bf16[1,2048,128]{2,1,0:T(8,128)(2,1)S(1)} %maximum_bitcast_fusion) | data formatting | bytes 1048576 | tf_op jit(solution)/shard_map/while/body/jit(dynamic_update_index_in_dim)/broadcast_in_dim | solution.py:167
  229.4 13.7 %reduce = bf16[2048,128]{1,0:T(8,128)(2,1)} reduce(bf16[2048,1,128]{2,1,0:T(2,128)(2,1)} %bitcast.188, bf16[]{:T(256)} %broadcast.485), dimensions={1}, to_apply=%bitcast.178.reduce_sub_computation | reduce | bytes 1048578
  245.1 7.5 all-to-all-start.3
  289.7 143.6 %scatter_fusion = bf16[64,2,8,2048]{3,2,1,0:T(8,128)(2,1)} fusion(bf16[64,2,8,2048]{3,2,1,0:T(8,128)(2,1)} %broadcast_in_dim.180, s32[768]{0:T(1024)S(1)} %reshape.373, bf16[768,2048]{1,0:T(8,128)(2,1)} %reshape.375), kind=kCustom, calls=%fused_computation.8 | custom fusion | bytes 9446400 | tf_op jit(solution)/shard_map/scatter | solution.py:199
  440.1 106.9 %all_to_all.49 = bf16[128,1,2,8,2048]{4,3,2,1,0:T(8,128)(2,1)S(1)} all-to-all(bf16[128,1,2,8,2048]{4,3,2,1,0:T(8,128)(2,1)} %bitcast.180), channel_id=1, replica_groups=mesh['req'=4,'exp'=32] {'req','exp'}, dimensions={0} | all-to-all | bytes 16777216 | tf_op jit(solution)/shard_map/all_to_all | solution.py:210
  550.2 12.8 %fusion.9 = f32[128,2,8,704]{0,3,2,1:T(8,128)} fusion(bf16[128,1,2,8,2048]{4,3,2,1,0:T(8,128)(2,1)S(1)} %all_to_all.49, bf16[2048,704]{0,1:T(8,128)(2,1)S(1)} %copy-done.34), kind=kOutput, calls=%fused_computation.27 | convolution fusion | flops 5905580032 | bytes 17039360 | tf_op jit(solution)/shard_map/nsrkd,dsf->nsrkf/dot_general | solution.py:214
  563.0 27.3 %convert_bitcast_fusion = bf16[128,1,2,8,2048]{4,0,3,2,1:T(8,128)(2,1)} fusion(bf16[704,2048]{1,0:T(8,128)(2,1)S(1)} %copy-done, f32[128,2,8,704]{0,3,2,1:T(8,128)} %fusion.9, bf16[128,1,2,8,2048]{4,3,2,1,0:T(8,128)(2,1)} %copy-done.7, bf16[2048,704]{0,1:T(8,128)(2,1)} %param.31), kind=kOutput, calls=%fused_computation.32 | convolution fusion | flops 11824005120 | bytes 28311552 | tf_op jit(solution)/shard_map/nsrkf,sfd->nsrkd/dot_general | solution.py:217
  590.3 11.2 %copy.62 = bf16[128,1,2,8,2048]{4,3,2,1,0:T(8,128)(2,1)} copy(bf16[128,1,2,8,2048]{4,0,3,2,1:T(8,128)(2,1)} %convert_bitcast_fusion) | data formatting | bytes 16777216 | tf_op jit(solution)/shard_map/convert_element_type | solution.py:219
  610.5 8.7 %fusion.44 = bf16[1,2,4096,128]{3,2,1,0:T(8,128)(2,1)} fusion(s32[]{:T(128)S(6)} %select_n.213, bf16[2,2048,128]{2,1,0:T(8,128)(2,1)} %slice.118, bf16[1,2048,64]{2,1,0:T(8,128)(2,1)} %bitcast.190, bf16[1,2048,64]{2,1,0:T(8,128)(2,1)} %bitcast.191, bf16[1,2048,128]{2,1,0:T(8,128)(2,1)S(1)} %bitcast.185), kind=kLoop, calls=%fused_computation.80 | loop fusion | flops 16777216 | bytes 4194308 | tf_op jit(solution)/shard_map/while/body/jit(dynamic_update_index_in_dim)/broadcast_in_dim | solution.py:167
  626.4 85.9 %all-to-all-done.5 = bf16[128,1,2,8,2048]{4,3,2,1,0:T(8,128)(2,1)} async-done(((bf16[128,1,2,8,2048]{4,3,2,1,0:T(8,128)(2,1)}), bf16[128,1,2,8,2048]{4,3,2,1,0:T(8,128)(2,1)}, u32[]{:S(2)}, u32[]{:S(2)}) %all-to-all-start.5) | async-done | bytes 8388640 | tf_op jit(solution)/shard_map/all_to_all | solution.py:216
  712.4 9.6 %convert_reduce_fusion = f32[64,2,8,2048]{3,2,1,0:T(8,128)} fusion(bf16[64,2,2,8,2048]{4,3,2,1,0:T(8,128)(2,1)} %bitcast.179), kind=kLoop, calls=%fused_computation.10 | loop fusion | flops 6291456 | bytes 16777216 | tf_op jit(solution)/shard_map/reduce_sum | solution.py:228
  722.0 15.5 %gather_fusion.2 = f32[768,2048]{1,0:T(8,128)} fusion(f32[64,2,8,2048]{3,2,1,0:T(8,128)} %convert_reduce_fusion, s32[768]{0:T(1024)S(1)} %reshape.355), kind=kCustom, calls=%fused_computation.5 | custom fusion | bytes 12592128 | tf_op jit(solution)/shard_map/gather | solution.py:229
  737.5 8.1 %reshape.358 = f32[2,64,6,2048]{3,2,1,0:T(8,128)} reshape(f32[768,2048]{1,0:T(8,128)} %gather_fusion.2) | data formatting | bytes 12582912 | tf_op jit(solution)/shard_map/gather | solution.py:229
  (178 shorter events, 150.7 us)
Async XLA Ops:
  7.2 555.9 %copy-start = (bf16[704,2048]{1,0:T(8,128)(2,1)S(1)}, bf16[704,2048]{1,0:T(8,128)(2,1)}, u32[]{:S(2)}) copy-start(bf16[704,2048]{1,0:T(8,128)(2,1)} %param.33) | copy-start | bytes 8650756
  7.2 38.8 %all-gather.11.cloned.1.call-start = ((), (), s32[]{:S(2)}) async-start(), calls=%async_computation.9 | async-start | bytes 2621440 | tf_op jit(solution)/shard_map/all_gather | solution.py:133
  7.9 66.4 %all-gather.9.cloned.1.call-start = ((), (), s32[]{:S(2)}) async-start(), calls=%async_computation.8 | async-start | bytes 2621440 | tf_op jit(solution)/shard_map/all_gather | solution.py:132
  8.7 98.1 %all-gather.7.cloned.1.call-start = ((), (), s32[]{:S(2)}) async-start(), calls=%async_computation.7 | async-start | bytes 2621440 | tf_op jit(solution)/shard_map/all_gather | solution.py:131
  9.4 253.0 %all-gather.5.cloned.1.call-start = ((), (), s32[]{:S(2)}) async-start(), calls=%async_computation.6 | async-start | bytes 2621440 | tf_op jit(solution)/shard_map/all_gather | solution.py:130
  14.0 95.8 %copy-start.29 = (pred[2]{0:T(512)(128)(4,1)}, pred[2]{0:T(512)(128)(4,1)S(1)}, u32[]{:S(2)}) copy-start(pred[2]{0:T(512)(128)(4,1)S(1)} %get-tuple-element.42) | copy-start | bytes 10
  14.0 92.8 %copy-start.31 = (s32[1024]{0:T(1024)}, s32[1024]{0:T(1024)S(1)}, u32[]{:S(2)}) copy-start(s32[1024]{0:T(1024)S(1)} %pad_clamp_fusion) | copy-start | bytes 12292
  27.6 225.1 %copy-start.27 = (s32[2,64,6]{1,2,0:T(8,128)}, s32[2,64,6]{1,2,0:T(8,128)S(1)}, u32[]{:S(2)}) copy-start(s32[2,64,6]{1,2,0:T(8,128)S(1)} %broadcast_select_fusion.3) | copy-start | bytes 9220
  112.3 17.9 %all-to-all-start.1 = ((bf16[32,64,128]{2,1,0:T(8,128)(2,1)}), bf16[32,64,128]{2,1,0:T(8,128)(2,1)S(1)}, u32[]{:S(2)}, u32[]{:S(2)}) async-start(bf16[32,64,128]{2,1,0:T(8,128)(2,1)} %bitcast.195), calls=%async_computation.1 | async-start | bytes 1048576 | tf_op jit(solution)/shard_map/all_to_all | solution.py:149
  130.2 16.2 %all-to-all-start = ((bf16[32,64,128]{2,1,0:T(8,128)(2,1)}), bf16[32,64,128]{2,1,0:T(8,128)(2,1)}, u32[]{:S(2)}, u32[]{:S(2)}) async-start(bf16[32,64,128]{2,1,0:T(8,128)(2,1)} %bitcast.194), calls=%async_computation | async-start | bytes 1048576 | tf_op jit(solution)/shard_map/all_to_all | solution.py:142
  146.4 24.5 %all-to-all-start.2 = ((bf16[32,64,128]{2,1,0:T(8,128)(2,1)}), bf16[32,64,128]{2,1,0:T(8,128)(2,1)S(1)}, u32[]{:S(2)}, u32[]{:S(2)}) async-start(bf16[32,64,128]{2,1,0:T(8,128)(2,1)} %bitcast.193), calls=%async_computation.2 | async-start | bytes 1048576 | tf_op jit(solution)/shard_map/all_to_all | solution.py:156
  152.5 8.7 %copy-start.33 = (bf16[1,2,4,128]{3,2,1,0:T(4,128)(2,1)S(1)}, bf16[1,2,4,128]{3,2,1,0:T(4,128)(2,1)}, u32[]{:S(2)}) copy-start(bf16[1,2,4,128]{3,2,1,0:T(4,128)(2,1)} %param.27) | copy-start | bytes 6148
  152.5 8.9 %copy-start.15 = (pred[512,4096]{1,0:T(32,128)(4,1)S(1)}, pred[512,4096]{1,0:T(32,128)(4,1)}, u32[]{:S(2)}) copy-start(pred[512,4096]{1,0:T(32,128)(4,1)} %get-tuple-element.61) | copy-start | bytes 6291460
  152.6 8.9 %copy-start.17 = (pred[512,2048]{1,0:T(32,128)(4,1)S(1)}, pred[512,2048]{1,0:T(32,128)(4,1)}, u32[]{:S(2)}) copy-start(pred[512,2048]{1,0:T(32,128)(4,1)} %iota_compare_fusion.4) | copy-start | bytes 3145732
  152.6 8.9 %copy-start.18 = (bf16[4096,128]{1,0:T(8,128)(2,1)S(1)}, bf16[4096,128]{1,0:T(8,128)(2,1)}, u32[]{:S(2)}) copy-start(bf16[4096,128]{1,0:T(8,128)(2,1)} %get-tuple-element.45) | copy-start | bytes 3145732
  170.9 7.7 %copy-start.11 = (bf16[2048,64]{1,0:T(8,128)(2,1)S(1)}, bf16[2048,64]{1,0:T(8,128)(2,1)}, u32[]{:S(2)}) copy-start(bf16[2048,64]{1,0:T(8,128)(2,1)} %copy-done.10) | copy-start | bytes 786436
  171.0 7.7 %copy-start.13 = (bf16[2048,64]{1,0:T(8,128)(2,1)S(1)}, bf16[2048,64]{1,0:T(8,128)(2,1)}, u32[]{:S(2)}) copy-start(bf16[2048,64]{1,0:T(8,128)(2,1)} %copy-done.12) | copy-start | bytes 786436
  171.0 7.7 %copy-start.14 = (pred[512,4096]{1,0:T(32,128)(4,1)S(1)}, pred[512,4096]{1,0:T(32,128)(4,1)}, u32[]{:S(2)}) copy-start(pred[512,4096]{1,0:T(32,128)(4,1)} %get-tuple-element.60) | copy-start | bytes 6291460
  171.0 7.7 %copy-start.16 = (pred[512,2048]{1,0:T(32,128)(4,1)S(1)}, pred[512,2048]{1,0:T(32,128)(4,1)}, u32[]{:S(2)}) copy-start(pred[512,2048]{1,0:T(32,128)(4,1)} %iota_compare_fusion.5) | copy-start | bytes 3145732
  245.1 20.4 %all-to-all-start.3 = ((bf16[32,2,4096]{2,1,0:T(2,128)(2,1)}), bf16[32,2,4096]{2,1,0:T(2,128)(2,1)}, u32[]{:S(2)}, u32[]{:S(2)}) async-start(bf16[32,2,4096]{2,1,0:T(2,128)(2,1)} %reshape.397), calls=%async_computation.3 | async-start | bytes 1048576 | tf_op jit(solution)/shard_map/all_to_all | solution.py:173
  440.1 110.1 %copy-start.34 = (bf16[2048,704]{0,1:T(8,128)(2,1)S(1)}, bf16[2048,704]{0,1:T(8,128)(2,1)}, u32[]{:S(2)}) copy-start(bf16[2048,704]{0,1:T(8,128)(2,1)} %param.32) | copy-start | bytes 8650756
  601.6 110.8 %all-to-all-start.5 = ((bf16[128,1,2,8,2048]{4,3,2,1,0:T(8,128)(2,1)}), bf16[128,1,2,8,2048]{4,3,2,1,0:T(8,128)(2,1)}, u32[]{:S(2)}, u32[]{:S(2)}) async-start(bf16[128,1,2,8,2048]{4,3,2,1,0:T(8,128)(2,1)} %copy.62), calls=%async_computation.5 | async-start | bytes 16777216 | tf_op jit(solution)/shard_map/all_to_all | solution.py:216
  610.4 8.7 %copy-start.9 = (bf16[2,64,2048]{2,1,0:T(8,128)(2,1)S(1)}, bf16[2,64,2048]{2,1,0:T(8,128)(2,1)}, u32[]{:S(2)}) copy-start(bf16[2,64,2048]{2,1,0:T(8,128)(2,1)} %copy-done.8) | copy-start | bytes 1572868
  610.4 8.7 %copy-start.25 = (bf16[2048,64]{0,1:T(8,128)(2,1)S(1)}, bf16[2048,64]{0,1:T(8,128)(2,1)}, u32[]{:S(2)}) copy-start(bf16[2048,64]{0,1:T(8,128)(2,1)} %param.30) | copy-start | bytes 786436
  (20 other events, 87.3 us)
Sparse Core Ops, SparseCore 0:
  9.6 32.1 all-gather.10
  43.5 30.7 all-gather.8
  76.0 30.7 all-gather.6
  108.3 30.7 all-gather.4
where the time goes:
time: 772 us; the launch traced here: 760 us
  local copies, waits for them, and re-layouts  261 us (34%)
  waiting for transfers between devices  162 us (21%)
  blocking collectives  119 us (15%)
  other arithmetic  86.2 us (11%)
  matrix products  84.1 us (11%)
  starting transfers between devices  32.2 us (4%)
  between operations  15.8 us (2%)
    scatter x1, local copies, waits for them, and re-layouts, on_device(): buffer = jnp.zeros((experts_all, slots_here, most_slots, model_width), jn...  144 us
    all_to_all x1, blocking collectives, on_device(): lax.all_to_all(outgoing, ('req', 'exp'), split_axis=0, concat_axis=0, til...  107 us
    all_to_all x1, waiting for transfers between devices, on_device(): lax.all_to_all(jnp.einsum('nsrkf,sfd->nsrkd', active, down_local, preferr...  85.9 us
    all_gather x1, waiting for transfers between devices, on_device(): lax.all_gather(q_new, 'req', axis=0, tiled=True)  29.5 us
    dot_general x1, matrix products, on_device(): jnp.einsum('nsrkf,sfd->nsrkd', active, down_local, preferred_element_type...  27.3 us
    all_gather x1, waiting for transfers between devices, on_device(): lax.all_gather(k_new, 'req', axis=0, tiled=True)  26.1 us
    gather x2, local copies, waits for them, and re-layouts, on_device(): picked = summed[route_sel, slot_ids, ranks]  23.6 us
    dot_general x4, matrix products, attend_block(): jnp.einsum('qd,kd->qk', q_block, key_rows, preferred_element_type=jnp.flo...  23.1 us
  transfers between devices with their start and end apart: 9, of which 5 were waited for; matrix products, arithmetic and copies ran while one was open for 20% of the time, Pallas kernels for 0%

commit v1 on v0

--- a/solution.py
+++ b/solution.py
@@ -4,6 +4,12 @@
 from jax.sharding import PartitionSpec as P
 
 SPLIT = 2
+
+
+def gather_by_exchange(x, axis, dim):
+    length = lax.axis_size(axis)
+    repeats = [length if d == dim else 1 for d in range(x.ndim)]
+    return lax.all_to_all(jnp.tile(x, repeats), axis, split_axis=dim, concat_axis=dim, tiled=True)
 
 
 def for_sending(array):
@@ -128,7 +134,7 @@
     experts_all = router.shape[1]
     arrived = (
         lax.all_gather(hidden, "req", axis=0, tiled=True),
-        lax.all_gather(q_new, "req", axis=0, tiled=True),
+        gather_by_exchange(q_new, "req", 0),
         lax.all_gather(k_new, "req", axis=0, tiled=True),
         lax.all_gather(v_new, "req", axis=0, tiled=True),
         lax.all_gather(routes, "req", axis=0, tiled=True),

time: 772 us -> 756 us (0.979)
  waiting for transfers between devices: 162 us -> 109 us
  blocking collectives: 119 us -> 151 us
    all_gather x1, blocking collectives: 12.3 us -> 43.9 us  [on_device(): lax.all_gather(routes, 'req', axis=0, tiled=True)]
    all_gather x1 -> x0, waiting for transfers between devices: 29.5 us -> none  [on_device(): lax.all_gather(q_new, 'req', axis=0, tiled=True)]
    all_gather x1, waiting for transfers between devices: 26.1 us -> 2.94 us  [on_device(): lax.all_gather(k_new, 'req', axis=0, tiled=True)]
    unnamed x75 -> x81, local copies, waits for them, and re-layouts: 23 us -> 22.3 us
  transfers between devices with their start and end apart: 9 -> 9, of which waited for: 5 -> 4; matrix products, arithmetic and copies ran while one was open for 20% -> 21% of each run, Pallas kernels for 0% -> 0%
where the time goes in v1:
time: 756 us; the launch traced here: 744 us
  local copies, waits for them, and re-layouts  262 us (35%)
  blocking collectives  151 us (20%)
  waiting for transfers between devices  109 us (14%)
  other arithmetic  85.4 us (11%)
  matrix products  84.1 us (11%)
  starting transfers between devices  37 us (5%)
  between operations  15.8 us (2%)
    scatter x1, local copies, waits for them, and re-layouts, on_device(): buffer = jnp.zeros((experts_all, slots_here, most_slots, model_width), jn...  144 us
    all_to_all x1, blocking collectives, on_device(): lax.all_to_all(outgoing, ('req', 'exp'), split_axis=0, concat_axis=0, til...  107 us
    all_to_all x1, waiting for transfers between devices, on_device(): lax.all_to_all(jnp.einsum('nsrkf,sfd->nsrkd', active, down_local, preferr...  85.9 us
    all_gather x1, blocking collectives, on_device(): lax.all_gather(routes, 'req', axis=0, tiled=True)  43.9 us
    dot_general x1, matrix products, on_device(): jnp.einsum('nsrkf,sfd->nsrkd', active, down_local, preferred_element_type...  27.3 us
    gather x2, local copies, waits for them, and re-layouts, on_device(): picked = summed[route_sel, slot_ids, ranks]  23.6 us
    dot_general x4, matrix products, attend_block(): jnp.einsum('qd,kd->qk', q_block, key_rows, preferred_element_type=jnp.flo...  23.1 us
    unnamed x81, local copies, waits for them, and re-layouts  22.3 us
  transfers between devices with their start and end apart: 9, of which 4 were waited for; matrix products, arithmetic and copies ran while one was open for 21% of the time, Pallas kernels for 0%

profile of v1, /device:TPU:10, one launch (start us, length us, event | category | flops | bytes accessed | tf_op | source)
XLA Modules:
  0.0 744.2 jit_solution(15395177708270646481)
XLA Ops:
  20.0 43.9 %all_gather.15 = s32[8,64,6]{1,2,0:T(8,128)S(1)} all-gather(s32[2,64,6]{1,2,0:T(8,128)S(1)} %copy.55), channel_id=1, replica_groups=mesh['req'=4,'exp'=32] {'req'}, dimensions={0}, use_global_device_ids=true | all-gather | bytes 15360 | tf_op jit(solution)/shard_map/all_gather | solution.py:140
  74.5 8.4 %fusion.13 = (pred[512,4096]{1,0:T(32,128)(4,1)}, pred[512,4096]{1,0:T(32,128)(4,1)}, pred[512,4096]{1,0:T(32,128)(4,1)}, pred[512,4096]{1,0:T(32,128)(4,1)}) fusion(pred[4096]{0:T(1024)(128)(4,1)S(1)} %iota_compare_fusion.9, s32[512]{0:T(512)S(1)} %iota_add_fusion.2, s32[512]{0:T(512)S(1)} %get-tuple-element.90, s32[512]{0:T(512)S(1)} %get-tuple-element.89), kind=kLoop, calls=%fused_computation.37 | loop fusion | flops 16777216 | bytes 8398848 | tf_op jit(solution)/shard_map/while/body/eval_jaxpr/and | solution.py:46
  96.5 7.6 %all-to-all-start.2 = ((bf16[32,64,128]{2,1,0:T(8,128)(2,1)}), bf16[32,64,128]{2,1,0:T(8,128)(2,1)S(1)}, u32[]{:S(2)}, u32[]{:S(2)}) async-start(bf16[32,64,128]{2,1,0:T(8,128)(2,1)} %bitcast.197), calls=%async_computation.2 | async-start | bytes 1048576 | tf_op jit(solution)/shard_map/all_to_all | solution.py:155
  105.7 8.7 %all-to-all-done.2 = bf16[32,64,128]{2,1,0:T(8,128)(2,1)S(1)} async-done(((bf16[32,64,128]{2,1,0:T(8,128)(2,1)}), bf16[32,64,128]{2,1,0:T(8,128)(2,1)S(1)}, u32[]{:S(2)}, u32[]{:S(2)}) %all-to-all-start.2) | async-done | bytes 524320 | tf_op jit(solution)/shard_map/all_to_all | solution.py:155
  121.2 9.4 %all-to-all-done.1 = bf16[32,64,128]{2,1,0:T(8,128)(2,1)} async-done(((bf16[32,64,128]{2,1,0:T(8,128)(2,1)}), bf16[32,64,128]{2,1,0:T(8,128)(2,1)}, u32[]{:S(2)}, u32[]{:S(2)}) %all-to-all-start.1) | async-done | bytes 524320 | tf_op jit(solution)/shard_map/all_to_all | solution.py:148
  136.8 7.5 %fusion.78 = (bf16[2048,64]{1,0:T(8,128)(2,1)S(1)}, bf16[2048,64]{1,0:T(8,128)(2,1)S(1)}, bf16[2048,64]{1,0:T(8,128)(2,1)S(1)}, bf16[2048,64]{1,0:T(8,128)(2,1)S(1)}) fusion(f32[2048,128]{1,0:T(8,128)} %bitcast_convert_fusion, f32[64]{0:T(128)S(1)} %multiply_power_fusion, f32[2048]{0:T(1024)S(1)} %add_convert_fusion.1, f32[2048,128]{1,0:T(8,128)S(1)} %bitcast_convert_fusion.1), kind=kLoop, calls=%fused_computation.126 | loop fusion | flops 2228224 | bytes 3154176 | tf_op jit(solution)/shard_map/convert.7
  155.2 7.5 %fusion.19 = f32[512,128]{1,0:T(8,128)} fusion(f32[512,6144]{1,0:T(8,128)} %copy-done.2, f32[512]{0:T(512)S(1)} %max.37, bf16[2048,128]{1,0:T(8,128)(2,1)S(1)} %bitcast.182, bf16[4096,128]{1,0:T(8,128)(2,1)} %get-tuple-element.44), kind=kOutput, calls=%fused_computation.43 | convolution fusion | flops 814743552 | bytes 14419968 | tf_op jit(solution)/shard_map/while/body/eval_jaxpr/dot_general | solution.py:68
  171.1 8.4 %fusion.143 = (f32[512]{0:T(512)S(1)}, f32[512,6144]{1,0:T(8,128)S(1)}) fusion(bf16[512,128]{1,0:T(8,128)(2,1)S(1)} %copy-done.21, bf16[2048,64]{1,0:T(8,128)(2,1)} %copy-done.12, bf16[2048,64]{1,0:T(8,128)(2,1)S(1)} %copy-done.11, bf16[4096,128]{1,0:T(8,128)(2,1)} %get-tuple-element.45, pred[512,2048]{1,0:T(32,128)(4,1)} %iota_compare_fusion.6, ...), kind=kOutput, calls=%fused_computation.234 | convolution fusion | flops 822607360 | bytes 17434624 | tf_op jit(solution)/shard_map/while/body/eval_jaxpr/qd,kd->qk/dot_general | solution.py:52
  181.6 8.6 %fusion.145 = (f32[512]{0:T(512)S(1)}, f32[512,6144]{1,0:T(8,128)}) fusion(bf16[512,128]{1,0:T(8,128)(2,1)S(1)} %copy-done.20, bf16[2048,64]{1,0:T(8,128)(2,1)} %copy-done.12, bf16[2048,64]{1,0:T(8,128)(2,1)S(1)} %copy-done.11, bf16[4096,128]{1,0:T(8,128)(2,1)} %get-tuple-element.45, pred[512,2048]{1,0:T(32,128)(4,1)} %iota_compare_fusion.7, ...), kind=kOutput, calls=%fused_computation.236 | convolution fusion | flops 822607360 | bytes 17434624 | tf_op jit(solution)/shard_map/while/body/eval_jaxpr/qd,kd->qk/dot_general | solution.py:52
  204.2 8.9 %copy.87 = bf16[1,2048,128]{2,0,1:T(2,128)(2,1)} copy(bf16[1,2048,128]{2,1,0:T(8,128)(2,1)S(1)} %maximum_bitcast_fusion) | data formatting | bytes 1048576 | tf_op jit(solution)/shard_map/while/body/jit(dynamic_update_index_in_dim)/broadcast_in_dim | solution.py:173
  213.7 13.7 %reduce = bf16[2048,128]{1,0:T(8,128)(2,1)} reduce(bf16[2048,1,128]{2,1,0:T(2,128)(2,1)} %bitcast.190, bf16[]{:T(256)} %broadcast.488), dimensions={1}, to_apply=%bitcast.179.reduce_sub_computation | reduce | bytes 1048578
  229.3 7.5 %all-to-all-start.4 = ((bf16[32,2,4096]{2,1,0:T(2,128)(2,1)}), bf16[32,2,4096]{2,1,0:T(2,128)(2,1)}, u32[]{:S(2)}, u32[]{:S(2)}) async-start(bf16[32,2,4096]{2,1,0:T(2,128)(2,1)} %reshape.401), calls=%async_computation.4 | async-start | bytes 1048576 | tf_op jit(solution)/shard_map/all_to_all | solution.py:179
  273.9 143.6 %scatter_fusion = bf16[64,2,8,2048]{3,2,1,0:T(8,128)(2,1)} fusion(bf16[64,2,8,2048]{3,2,1,0:T(8,128)(2,1)} %broadcast_in_dim.180, s32[768]{0:T(1024)S(1)} %reshape.377, bf16[768,2048]{1,0:T(8,128)(2,1)} %reshape.379), kind=kCustom, calls=%fused_computation.8 | custom fusion | bytes 9446400 | tf_op jit(solution)/shard_map/scatter | solution.py:205
  417.5 6.8 broadcast_in_dim.183
  424.2 106.8 %all_to_all.54 = bf16[128,1,2,8,2048]{4,3,2,1,0:T(8,128)(2,1)S(1)} all-to-all(bf16[128,1,2,8,2048]{4,3,2,1,0:T(8,128)(2,1)} %bitcast.181), channel_id=1, replica_groups=mesh['req'=4,'exp'=32] {'req','exp'}, dimensions={0} | all-to-all | bytes 16777216 | tf_op jit(solution)/shard_map/all_to_all | solution.py:216
  534.3 12.8 %fusion.9 = f32[128,2,8,704]{0,3,2,1:T(8,128)} fusion(bf16[128,1,2,8,2048]{4,3,2,1,0:T(8,128)(2,1)S(1)} %all_to_all.54, bf16[2048,704]{0,1:T(8,128)(2,1)S(1)} %copy-done.36), kind=kOutput, calls=%fused_computation.27 | convolution fusion | flops 5905580032 | bytes 17039360 | tf_op jit(solution)/shard_map/nsrkd,dsf->nsrkf/dot_general | solution.py:220
  547.1 27.3 %convert_bitcast_fusion = bf16[128,1,2,8,2048]{4,0,3,2,1:T(8,128)(2,1)} fusion(bf16[704,2048]{1,0:T(8,128)(2,1)S(1)} %copy-done, f32[128,2,8,704]{0,3,2,1:T(8,128)} %fusion.9, bf16[128,1,2,8,2048]{4,3,2,1,0:T(8,128)(2,1)} %copy-done.7, bf16[2048,704]{0,1:T(8,128)(2,1)} %param.31), kind=kOutput, calls=%fused_computation.32 | convolution fusion | flops 11824005120 | bytes 28311552 | tf_op jit(solution)/shard_map/nsrkf,sfd->nsrkd/dot_general | solution.py:223
  574.4 11.2 %copy.62 = bf16[128,1,2,8,2048]{4,3,2,1,0:T(8,128)(2,1)} copy(bf16[128,1,2,8,2048]{4,0,3,2,1:T(8,128)(2,1)} %convert_bitcast_fusion) | data formatting | bytes 16777216 | tf_op jit(solution)/shard_map/convert_element_type | solution.py:225
  594.5 8.7 %fusion.44 = bf16[1,2,4096,128]{3,2,1,0:T(8,128)(2,1)} fusion(s32[]{:T(128)S(6)} %select_n.213, bf16[2,2048,128]{2,1,0:T(8,128)(2,1)} %slice.118, bf16[1,2048,64]{2,1,0:T(8,128)(2,1)} %bitcast.192, bf16[1,2048,64]{2,1,0:T(8,128)(2,1)} %bitcast.193, bf16[1,2048,128]{2,1,0:T(8,128)(2,1)S(1)} %bitcast.186), kind=kLoop, calls=%fused_computation.80 | loop fusion | flops 16777216 | bytes 4194308 | tf_op jit(solution)/shard_map/while/body/jit(dynamic_update_index_in_dim)/broadcast_in_dim | solution.py:173
  610.5 85.9 %all-to-all-done.6 = bf16[128,1,2,8,2048]{4,3,2,1,0:T(8,128)(2,1)} async-done(((bf16[128,1,2,8,2048]{4,3,2,1,0:T(8,128)(2,1)}), bf16[128,1,2,8,2048]{4,3,2,1,0:T(8,128)(2,1)}, u32[]{:S(2)}, u32[]{:S(2)}) %all-to-all-start.6) | async-done | bytes 8388640 | tf_op jit(solution)/shard_map/all_to_all | solution.py:222
  696.4 9.6 %convert_reduce_fusion = f32[64,2,8,2048]{3,2,1,0:T(8,128)} fusion(bf16[64,2,2,8,2048]{4,3,2,1,0:T(8,128)(2,1)} %bitcast.180), kind=kLoop, calls=%fused_computation.10 | loop fusion | flops 6291456 | bytes 16777216 | tf_op jit(solution)/shard_map/reduce_sum | solution.py:234
  706.0 15.5 %gather_fusion.2 = f32[768,2048]{1,0:T(8,128)} fusion(f32[64,2,8,2048]{3,2,1,0:T(8,128)} %convert_reduce_fusion, s32[768]{0:T(1024)S(1)} %reshape.359), kind=kCustom, calls=%fused_computation.5 | custom fusion | bytes 12592128 | tf_op jit(solution)/shard_map/gather | solution.py:235
  721.5 8.1 %reshape.362 = f32[2,64,6,2048]{3,2,1,0:T(8,128)} reshape(f32[768,2048]{1,0:T(8,128)} %gather_fusion.2) | data formatting | bytes 12582912 | tf_op jit(solution)/shard_map/gather | solution.py:235
  729.6 6.7 multiply_reduce_fusion
  (184 shorter events, 145.3 us)
Async XLA Ops:
  7.2 539.9 %copy-start = (bf16[704,2048]{1,0:T(8,128)(2,1)S(1)}, bf16[704,2048]{1,0:T(8,128)(2,1)}, u32[]{:S(2)}) copy-start(bf16[704,2048]{1,0:T(8,128)(2,1)} %param.33) | copy-start | bytes 8650756
  7.2 10.1 %copy-start.37 = (s32[8]{0:T(128)S(1)}, s32[8]{0:T(128)}, u32[]{:S(2)}) copy-start(s32[8]{0:T(128)} %param.25) | copy-start | bytes 100
  7.2 77.9 %all-gather.8.cloned.1.call-start = ((), (), s32[]{:S(2)}) async-start(), calls=%async_computation.9 | async-start | bytes 2621440 | tf_op jit(solution)/shard_map/all_gather | solution.py:139
  7.9 83.1 %all-gather.6.cloned.1.call-start = ((), (), s32[]{:S(2)}) async-start(), calls=%async_computation.8 | async-start | bytes 2621440 | tf_op jit(solution)/shard_map/all_gather | solution.py:138
  8.7 11.2 %copy-start.35 = (s32[8]{0:T(128)S(1)}, s32[8]{0:T(128)}, u32[]{:S(2)}) copy-start(s32[8]{0:T(128)} %param.24) | copy-start | bytes 100
  8.7 11.2 %copy-start.34 = (s32[2,64,6]{1,0,2:T(2,128)S(1)}, s32[2,64,6]{1,0,2:T(2,128)}, u32[]{:S(2)}) copy-start(s32[2,64,6]{1,0,2:T(2,128)} %param.23) | copy-start | bytes 9220
  11.6 71.2 %all-to-all-start = ((bf16[8,16,64,128]{3,2,1,0:T(8,128)(2,1)}), bf16[8,16,64,128]{3,2,1,0:T(8,128)(2,1)}, u32[]{:S(2)}, u32[]{:S(2)}) async-start(bf16[8,16,64,128]{3,2,1,0:T(8,128)(2,1)} %bitcast.188), calls=%async_computation | async-start | bytes 4194304 | tf_op jit(solution)/shard_map/all_to_all | solution.py:12
  16.5 230.1 %all-gather.4.cloned.1.call-start = ((), (), s32[]{:S(2)}) async-start(), calls=%async_computation.7 | async-start | bytes 2621440 | tf_op jit(solution)/shard_map/all_gather | solution.py:136
  19.9 74.1 %copy-start.29 = (pred[2]{0:T(512)(128)(4,1)}, pred[2]{0:T(512)(128)(4,1)S(1)}, u32[]{:S(2)}) copy-start(pred[2]{0:T(512)(128)(4,1)S(1)} %get-tuple-element.42) | copy-start | bytes 10
  19.9 71.1 %copy-start.31 = (s32[1024]{0:T(1024)}, s32[1024]{0:T(1024)S(1)}, u32[]{:S(2)}) copy-start(s32[1024]{0:T(1024)S(1)} %pad_clamp_fusion) | copy-start | bytes 12292
  64.5 172.4 %copy-start.27 = (s32[2,64,6]{1,2,0:T(8,128)}, s32[2,64,6]{1,2,0:T(8,128)S(1)}, u32[]{:S(2)}) copy-start(s32[2,64,6]{1,2,0:T(8,128)S(1)} %broadcast_select_fusion.3) | copy-start | bytes 9220
  96.5 17.9 %all-to-all-start.2 = ((bf16[32,64,128]{2,1,0:T(8,128)(2,1)}), bf16[32,64,128]{2,1,0:T(8,128)(2,1)S(1)}, u32[]{:S(2)}, u32[]{:S(2)}) async-start(bf16[32,64,128]{2,1,0:T(8,128)(2,1)} %bitcast.197), calls=%async_computation.2 | async-start | bytes 1048576 | tf_op jit(solution)/shard_map/all_to_all | solution.py:155
  114.5 16.2 %all-to-all-start.1 = ((bf16[32,64,128]{2,1,0:T(8,128)(2,1)}), bf16[32,64,128]{2,1,0:T(8,128)(2,1)}, u32[]{:S(2)}, u32[]{:S(2)}) async-start(bf16[32,64,128]{2,1,0:T(8,128)(2,1)} %bitcast.196), calls=%async_computation.1 | async-start | bytes 1048576 | tf_op jit(solution)/shard_map/all_to_all | solution.py:148
  130.7 24.5 %all-to-all-start.3 = ((bf16[32,64,128]{2,1,0:T(8,128)(2,1)}), bf16[32,64,128]{2,1,0:T(8,128)(2,1)S(1)}, u32[]{:S(2)}, u32[]{:S(2)}) async-start(bf16[32,64,128]{2,1,0:T(8,128)(2,1)} %bitcast.195), calls=%async_computation.3 | async-start | bytes 1048576 | tf_op jit(solution)/shard_map/all_to_all | solution.py:162
  136.8 8.7 %copy-start.33 = (bf16[1,2,4,128]{3,2,1,0:T(4,128)(2,1)S(1)}, bf16[1,2,4,128]{3,2,1,0:T(4,128)(2,1)}, u32[]{:S(2)}) copy-start(bf16[1,2,4,128]{3,2,1,0:T(4,128)(2,1)} %param.27) | copy-start | bytes 6148
  136.8 8.8 %copy-start.15 = (pred[512,4096]{1,0:T(32,128)(4,1)S(1)}, pred[512,4096]{1,0:T(32,128)(4,1)}, u32[]{:S(2)}) copy-start(pred[512,4096]{1,0:T(32,128)(4,1)} %get-tuple-element.61) | copy-start | bytes 6291460
  136.8 8.8 %copy-start.17 = (pred[512,2048]{1,0:T(32,128)(4,1)S(1)}, pred[512,2048]{1,0:T(32,128)(4,1)}, u32[]{:S(2)}) copy-start(pred[512,2048]{1,0:T(32,128)(4,1)} %iota_compare_fusion.4) | copy-start | bytes 3145732
  136.8 8.8 %copy-start.18 = (bf16[4096,128]{1,0:T(8,128)(2,1)S(1)}, bf16[4096,128]{1,0:T(8,128)(2,1)}, u32[]{:S(2)}) copy-start(bf16[4096,128]{1,0:T(8,128)(2,1)} %get-tuple-element.45) | copy-start | bytes 3145732
  155.1 7.7 %copy-start.11 = (bf16[2048,64]{1,0:T(8,128)(2,1)S(1)}, bf16[2048,64]{1,0:T(8,128)(2,1)}, u32[]{:S(2)}) copy-start(bf16[2048,64]{1,0:T(8,128)(2,1)} %copy-done.10) | copy-start | bytes 786436
  229.3 20.4 %all-to-all-start.4 = ((bf16[32,2,4096]{2,1,0:T(2,128)(2,1)}), bf16[32,2,4096]{2,1,0:T(2,128)(2,1)}, u32[]{:S(2)}, u32[]{:S(2)}) async-start(bf16[32,2,4096]{2,1,0:T(2,128)(2,1)} %reshape.401), calls=%async_computation.4 | async-start | bytes 1048576 | tf_op jit(solution)/shard_map/all_to_all | solution.py:179
  424.2 110.0 %copy-start.36 = (bf16[2048,704]{0,1:T(8,128)(2,1)S(1)}, bf16[2048,704]{0,1:T(8,128)(2,1)}, u32[]{:S(2)}) copy-start(bf16[2048,704]{0,1:T(8,128)(2,1)} %param.32) | copy-start | bytes 8650756
  585.7 110.8 %all-to-all-start.6 = ((bf16[128,1,2,8,2048]{4,3,2,1,0:T(8,128)(2,1)}), bf16[128,1,2,8,2048]{4,3,2,1,0:T(8,128)(2,1)}, u32[]{:S(2)}, u32[]{:S(2)}) async-start(bf16[128,1,2,8,2048]{4,3,2,1,0:T(8,128)(2,1)} %copy.62), calls=%async_computation.6 | async-start | bytes 16777216 | tf_op jit(solution)/shard_map/all_to_all | solution.py:222
  594.5 8.7 %copy-start.9 = (bf16[2,64,2048]{2,1,0:T(8,128)(2,1)S(1)}, bf16[2,64,2048]{2,1,0:T(8,128)(2,1)}, u32[]{:S(2)}) copy-start(bf16[2,64,2048]{2,1,0:T(8,128)(2,1)} %copy-done.8) | copy-start | bytes 1572868
  594.5 8.7 %copy-start.25 = (bf16[2048,64]{0,1:T(8,128)(2,1)S(1)}, bf16[2048,64]{0,1:T(8,128)(2,1)}, u32[]{:S(2)}) copy-start(bf16[2048,64]{0,1:T(8,128)(2,1)} %param.30) | copy-start | bytes 786436
  (23 other events, 110.4 us)
Sparse Core Ops, SparseCore 0:
  9.7 47.9 all-gather.7
  59.3 31.7 all-gather.5
  92.7 30.7 all-gather.3
